TPU v7x, 32 devices: a whole 2x2x4 slice. The times are simulated.
32 devices in a mesh: wide: 16 (over z, y, x), narrow: 2 (over core).
Axes of the slice: x: 2, y: 2, z: 4, core: 2. Of those that a mesh axis runs over, the one named last changes fastest.
Arguments:
- activations: bfloat16 [16384, 1024], P(('wide', 'narrow')), may hold values from -6 to 6
- segment_ids: int32 [16384], P(('wide', 'narrow')), may hold values from -1 to 511, as said below
- cotangent: bfloat16 [16384, 1024], P(('wide', 'narrow')), may hold values from -6 to 6
- querymat: bfloat16 [1024, 1024], P(('wide', 'narrow')), may hold values from -0.1875 to 0.1875
- keymat: bfloat16 [1024, 1024], P(('wide', 'narrow')), may hold values from -0.1875 to 0.1875
- valuemat: bfloat16 [1024, 1024], P(('wide', 'narrow')), may hold values from -0.1875 to 0.1875
- outmat: bfloat16 [1024, 1024], P(('wide', 'narrow')), may hold values from -0.1875 to 0.1875
- upmatrix: bfloat16 [1024, 4096], P(('wide', 'narrow')), may hold values from -0.1875 to 0.1875
- downmatrix: bfloat16 [4096, 1024], P(('wide', 'narrow')), may hold values from -0.09375 to 0.09375
- querybias: bfloat16 [1024], P(('wide', 'narrow')), may hold values from -3 to 3
- keybias: bfloat16 [1024], P(('wide', 'narrow')), may hold values from -3 to 3
- valuebias: bfloat16 [1024], P(('wide', 'narrow')), may hold values from -3 to 3
- outbias: bfloat16 [1024], P(('wide', 'narrow')), may hold values from -3 to 3
- upbias: bfloat16 [4096], P(('wide', 'narrow')), may hold values from -3 to 3
- downbias: bfloat16 [1024], P(('wide', 'narrow')), may hold values from -3 to 3
- firstgain: bfloat16 [1024], P(('wide', 'narrow')), may hold values from 0.099609375 to 1.8984375
- secondgain: bfloat16 [1024], P(('wide', 'narrow')), may hold values from 0.099609375 to 1.8984375
- thirdgain: bfloat16 [1024], P(('wide', 'narrow')), may hold values from 0.099609375 to 1.8984375
- fourthgain: bfloat16 [1024], P(('wide', 'narrow')), may hold values from 0.099609375 to 1.8984375
Outputs:
- layer_out: bfloat16 [16384, 1024], P(('wide', 'narrow'))
- input_gradient: float32 [16384, 1024], P(('wide', 'narrow'))
- querymat_gradient: float32 [1024, 1024], P(('wide', 'narrow'))
- keymat_gradient: float32 [1024, 1024], P(('wide', 'narrow'))
- valuemat_gradient: float32 [1024, 1024], P(('wide', 'narrow'))
- outmat_gradient: float32 [1024, 1024], P(('wide', 'narrow'))
- upmatrix_gradient: float32 [1024, 4096], P(('wide', 'narrow'))
- downmatrix_gradient: float32 [4096, 1024], P(('wide', 'narrow'))
- querybias_gradient: float32 [1024], P(('wide', 'narrow'))
- keybias_gradient: float32 [1024], P(('wide', 'narrow'))
- valuebias_gradient: float32 [1024], P(('wide', 'narrow'))
- outbias_gradient: float32 [1024], P(('wide', 'narrow'))
- upbias_gradient: float32 [4096], P(('wide', 'narrow'))
- downbias_gradient: float32 [1024], P(('wide', 'narrow'))
- firstgain_gradient: float32 [1024], P(('wide', 'narrow'))
- secondgain_gradient: float32 [1024], P(('wide', 'narrow'))
- thirdgain_gradient: float32 [1024], P(('wide', 'narrow'))
- fourthgain_gradient: float32 [1024], P(('wide', 'narrow'))
- output_power: float32 [], replicated
Inputs may be any that keep to these rules, and one draw needn't show every extreme that they name: `segment_ids`: in each packed row of 512 slots the ids of the used slots start at 0 and never fall, each sequence being a run of equal ids; the used slots come first, 128 or more of them, and the rest hold -1; some row holds one sequence of 512 tokens, and some row holds 512 sequences of one token.
All inputs are finite; a program needn't handle non-finite values.
Results may differ from a plain program's by a relative error of at most 0.019.
Values may be sent and summed in bfloat16 or wider, within the bound.
No kernel may reach another device: no remote copies, remote signals or barrier semaphores. Data moves between devices by JAX's collectives and lax.ppermute only.
A program may use at most 256 MiB of HBM per device.

v0:
```python
import jax
import jax.numpy as jnp
from jax import lax
from jax.sharding import PartitionSpec as P

HEAD = 64


def rms_norm(values, gain):
    return values * lax.rsqrt(jnp.mean(values * values, axis=-1, keepdims=True) + 1e-06) * gain


def rotate(values, cosine, sine):
    midpoint = values.shape[-1] // 2
    first_half = values[..., :midpoint]
    second_half = values[..., midpoint:]
    return jnp.concatenate(
        [first_half * cosine - second_half * sine, first_half * sine + second_half * cosine],
        axis=-1,
    )


def positions_of(segment):
    places = jnp.arange(segment.shape[0])
    matching = segment[:, None] == segment[None, :]
    earlier = places[None, :] < places[:, None]
    return jnp.sum(jnp.logical_and(matching, earlier).astype(jnp.int32), axis=1)


def angle_tables(segment):
    places = positions_of(segment).astype(jnp.float32)
    midpoint = HEAD // 2
    inverse = 10000.0 ** (-jnp.arange(midpoint).astype(jnp.float32) * 2.0 / HEAD)
    angles = places[:, None] * inverse[None, :]
    return (jnp.cos(angles)[:, None, :], jnp.sin(angles)[:, None, :])


def key_mask(segment):
    places = jnp.arange(segment.shape[0])
    matching = segment[:, None] == segment[None, :]
    allowed = matching & (segment[None, :] >= 0) & (places[None, :] <= places[:, None])
    return allowed | (places[None, :] == places[:, None])


def contract_rows(left, right):
    return lax.dot_general(
        left, right, (((0,), (0,)), ((), ())), preferred_element_type=jnp.float32
    )


def times_transpose(left, right):
    return lax.dot_general(
        left, right, (((1,), (1,)), ((), ())), preferred_element_type=jnp.float32
    )


def product(left, right):
    return jnp.dot(left, right, preferred_element_type=jnp.float32)


def column_sums(values):
    return jnp.sum(values.astype(jnp.float32), axis=0)


def masked_scores(query_rot, key_rot, allowed):
    scores = (
        jnp.einsum("qhd,khd->hqk", query_rot, key_rot, preferred_element_type=jnp.float32) * 0.125
    )
    return jnp.where(allowed[None], scores, -1e30)


def shards(
    activations,
    segment_ids,
    cotangent,
    querymat,
    keymat,
    valuemat,
    outmat,
    upmatrix,
    downmatrix,
    querybias,
    keybias,
    valuebias,
    outbias,
    upbias,
    downbias,
    firstgain,
    secondgain,
    thirdgain,
    fourthgain,
):
    gathered = (
        lax.all_gather(querymat, ("wide", "narrow"), axis=0, tiled=True),
        lax.all_gather(keymat, ("wide", "narrow"), axis=0, tiled=True),
        lax.all_gather(valuemat, ("wide", "narrow"), axis=0, tiled=True),
        lax.all_gather(outmat, ("wide", "narrow"), axis=0, tiled=True),
        lax.all_gather(upmatrix, ("wide", "narrow"), axis=0, tiled=True),
        lax.all_gather(downmatrix, ("wide", "narrow"), axis=0, tiled=True),
        lax.all_gather(querybias, ("wide", "narrow"), axis=0, tiled=True),
        lax.all_gather(keybias, ("wide", "narrow"), axis=0, tiled=True),
        lax.all_gather(valuebias, ("wide", "narrow"), axis=0, tiled=True),
        lax.all_gather(outbias, ("wide", "narrow"), axis=0, tiled=True),
        lax.all_gather(upbias, ("wide", "narrow"), axis=0, tiled=True),
        lax.all_gather(downbias, ("wide", "narrow"), axis=0, tiled=True),
        lax.all_gather(firstgain, ("wide", "narrow"), axis=0, tiled=True),
        lax.all_gather(secondgain, ("wide", "narrow"), axis=0, tiled=True),
        lax.all_gather(thirdgain, ("wide", "narrow"), axis=0, tiled=True),
        lax.all_gather(fourthgain, ("wide", "narrow"), axis=0, tiled=True),
    )
    (
        full_query,
        full_key,
        full_value,
        full_output,
        full_up,
        full_down,
        bias_query,
        bias_key,
        bias_value,
        bias_output,
        bias_up,
        bias_down,
        gain_first,
        gain_second,
        gain_third,
        gain_fourth,
    ) = gathered
    length = activations.shape[0]
    heads = full_query.shape[1] // HEAD
    width = full_query.shape[1]
    inputs = activations.astype(jnp.float32)
    cosine, sine = angle_tables(segment_ids)
    allowed = key_mask(segment_ids)
    valid_row = (segment_ids >= 0).astype(jnp.float32)
    normed_in, pull_first = jax.vjp(rms_norm, inputs, gain_first.astype(jnp.float32))
    normed_low = normed_in.astype(jnp.bfloat16)
    queries = product(normed_low, full_query) + bias_query.astype(jnp.float32)
    keys_pre = product(normed_low, full_key) + bias_key.astype(jnp.float32)
    values_pre = product(normed_low, full_value) + bias_value.astype(jnp.float32)
    query_rot = rotate(queries.reshape(length, heads, HEAD), cosine, sine).astype(jnp.bfloat16)
    key_rot = rotate(keys_pre.reshape(length, heads, HEAD), cosine, sine).astype(jnp.bfloat16)
    value_low = values_pre.reshape(length, heads, HEAD).astype(jnp.bfloat16)
    scores = masked_scores(query_rot, key_rot, allowed)
    peak = jnp.max(scores, axis=-1, keepdims=True)
    exponent = jnp.exp(scores - peak)
    totals = jnp.sum(exponent, axis=-1, keepdims=True)
    logsum = peak + jnp.log(totals)
    probs = exponent / totals
    mixed = jnp.einsum(
        "hqk,khd->qhd", probs.astype(jnp.bfloat16), value_low, preferred_element_type=jnp.float32
    )
    mixed_low = mixed.reshape(length, width).astype(jnp.bfloat16)
    attended = product(mixed_low, full_output) + bias_output.astype(jnp.float32)
    normed_att, pull_second = jax.vjp(rms_norm, attended, gain_second.astype(jnp.float32))
    middle = inputs + normed_att
    normed_mid, pull_third = jax.vjp(rms_norm, middle, gain_third.astype(jnp.float32))
    normed_mid_low = normed_mid.astype(jnp.bfloat16)
    expanded = product(normed_mid_low, full_up) + bias_up.astype(jnp.float32)
    activated_f, pull_gelu = jax.vjp(jax.nn.gelu, expanded)
    activated = activated_f.astype(jnp.bfloat16)
    contracted = product(activated, full_down) + bias_down.astype(jnp.float32)
    local_power = jnp.sum(valid_row * jnp.mean(contracted * contracted, axis=-1))
    power_total = lax.psum(local_power, ("wide", "narrow"))
    output_power = power_total / (length * lax.axis_size("wide") * lax.axis_size("narrow"))
    normed_out, pull_fourth = jax.vjp(rms_norm, contracted, gain_fourth.astype(jnp.float32))
    layer_out = (middle + normed_out).astype(jnp.bfloat16)
    again = (
        lax.all_gather(querymat, ("wide", "narrow"), axis=0, tiled=True),
        lax.all_gather(keymat, ("wide", "narrow"), axis=0, tiled=True),
        lax.all_gather(valuemat, ("wide", "narrow"), axis=0, tiled=True),
        lax.all_gather(outmat, ("wide", "narrow"), axis=0, tiled=True),
        lax.all_gather(upmatrix, ("wide", "narrow"), axis=0, tiled=True),
        lax.all_gather(downmatrix, ("wide", "narrow"), axis=0, tiled=True),
        lax.all_gather(querybias, ("wide", "narrow"), axis=0, tiled=True),
        lax.all_gather(keybias, ("wide", "narrow"), axis=0, tiled=True),
        lax.all_gather(valuebias, ("wide", "narrow"), axis=0, tiled=True),
        lax.all_gather(outbias, ("wide", "narrow"), axis=0, tiled=True),
        lax.all_gather(upbias, ("wide", "narrow"), axis=0, tiled=True),
        lax.all_gather(downbias, ("wide", "narrow"), axis=0, tiled=True),
        lax.all_gather(firstgain, ("wide", "narrow"), axis=0, tiled=True),
        lax.all_gather(secondgain, ("wide", "narrow"), axis=0, tiled=True),
        lax.all_gather(thirdgain, ("wide", "narrow"), axis=0, tiled=True),
        lax.all_gather(fourthgain, ("wide", "narrow"), axis=0, tiled=True),
    )
    back_query, back_key, back_value, back_output, back_up, back_down = (
        again[0],
        again[1],
        again[2],
        again[3],
        again[4],
        again[5],
    )
    seed = cotangent.astype(jnp.float32) * valid_row[:, None]
    d_contracted_f, fourth_slope = pull_fourth(seed)
    d_contracted = d_contracted_f.astype(jnp.bfloat16)
    down_slope = contract_rows(activated, d_contracted)
    down_bias_slope = column_sums(d_contracted)
    d_activated = times_transpose(d_contracted, back_down)
    d_expanded = pull_gelu(d_activated)[0].astype(jnp.bfloat16)
    up_slope = contract_rows(normed_mid_low, d_expanded)
    up_bias_slope = column_sums(d_expanded)
    d_normed_mid = times_transpose(d_expanded, back_up)
    d_middle_part, third_slope = pull_third(d_normed_mid)
    d_middle = seed + d_middle_part
    d_attended_f, second_slope = pull_second(d_middle)
    d_attended = d_attended_f.astype(jnp.bfloat16)
    output_slope = contract_rows(mixed_low, d_attended)
    output_bias_slope = column_sums(d_attended)
    d_mixed = (
        times_transpose(d_attended, back_output).astype(jnp.bfloat16).reshape(length, heads, HEAD)
    )
    probs_again = jnp.exp(masked_scores(query_rot, key_rot, allowed) - logsum)
    d_values = jnp.einsum(
        "hqk,qhd->khd",
        probs_again.astype(jnp.bfloat16),
        d_mixed,
        preferred_element_type=jnp.float32,
    )
    d_probs = jnp.einsum("qhd,khd->hqk", d_mixed, value_low, preferred_element_type=jnp.float32)
    row_terms = jnp.sum(probs_again * d_probs, axis=-1, keepdims=True)
    d_scores = (probs_again * (d_probs - row_terms)).astype(jnp.bfloat16)
    d_query_rot = (
        jnp.einsum("hqk,khd->qhd", d_scores, key_rot, preferred_element_type=jnp.float32) * 0.125
    )
    d_key_rot = (
        jnp.einsum("hqk,qhd->khd", d_scores, query_rot, preferred_element_type=jnp.float32) * 0.125
    )
    d_queries = rotate(d_query_rot, cosine, -sine).reshape(length, width).astype(jnp.bfloat16)
    d_keys = rotate(d_key_rot, cosine, -sine).reshape(length, width).astype(jnp.bfloat16)
    d_values_low = d_values.reshape(length, width).astype(jnp.bfloat16)
    query_slope = contract_rows(normed_low, d_queries)
    key_slope = contract_rows(normed_low, d_keys)
    value_slope = contract_rows(normed_low, d_values_low)
    query_bias_slope = column_sums(d_queries)
    key_bias_slope = column_sums(d_keys)
    value_bias_slope = column_sums(d_values_low)
    d_normed = (
        times_transpose(d_queries, back_query)
        + times_transpose(d_keys, back_key)
        + times_transpose(d_values_low, back_value)
    )
    d_inputs_part, first_slope = pull_first(d_normed)
    input_gradient = d_middle + d_inputs_part
    summed = (
        lax.psum_scatter(query_slope, ("wide", "narrow"), scatter_dimension=0, tiled=True),
        lax.psum_scatter(key_slope, ("wide", "narrow"), scatter_dimension=0, tiled=True),
        lax.psum_scatter(value_slope, ("wide", "narrow"), scatter_dimension=0, tiled=True),
        lax.psum_scatter(output_slope, ("wide", "narrow"), scatter_dimension=0, tiled=True),
        lax.psum_scatter(query_bias_slope, ("wide", "narrow"), scatter_dimension=0, tiled=True),
        lax.psum_scatter(key_bias_slope, ("wide", "narrow"), scatter_dimension=0, tiled=True),
        lax.psum_scatter(value_bias_slope, ("wide", "narrow"), scatter_dimension=0, tiled=True),
        lax.psum_scatter(output_bias_slope, ("wide", "narrow"), scatter_dimension=0, tiled=True),
        lax.psum_scatter(first_slope, ("wide", "narrow"), scatter_dimension=0, tiled=True),
        lax.psum_scatter(second_slope, ("wide", "narrow"), scatter_dimension=0, tiled=True),
        lax.psum_scatter(up_slope, ("wide", "narrow"), scatter_dimension=0, tiled=True),
        lax.psum_scatter(down_slope, ("wide", "narrow"), scatter_dimension=0, tiled=True),
        lax.psum_scatter(up_bias_slope, ("wide", "narrow"), scatter_dimension=0, tiled=True),
        lax.psum_scatter(down_bias_slope, ("wide", "narrow"), scatter_dimension=0, tiled=True),
        lax.psum_scatter(third_slope, ("wide", "narrow"), scatter_dimension=0, tiled=True),
        lax.psum_scatter(fourth_slope, ("wide", "narrow"), scatter_dimension=0, tiled=True),
    )
    attention_sums = summed[:10]
    feed_sums = summed[10:]
    return (
        layer_out,
        input_gradient,
        attention_sums[0],
        attention_sums[1],
        attention_sums[2],
        attention_sums[3],
        feed_sums[0],
        feed_sums[1],
        attention_sums[4],
        attention_sums[5],
        attention_sums[6],
        attention_sums[7],
        feed_sums[2],
        feed_sums[3],
        attention_sums[8],
        attention_sums[9],
        feed_sums[4],
        feed_sums[5],
        output_power,
    )


def solution(mesh):
    placed = (
        P(("wide", "narrow"), None),
        P(("wide", "narrow")),
        P(("wide", "narrow"), None),
        P(("wide", "narrow"), None),
        P(("wide", "narrow"), None),
        P(("wide", "narrow"), None),
        P(("wide", "narrow"), None),
        P(("wide", "narrow"), None),
        P(("wide", "narrow"), None),
        P(("wide", "narrow")),
        P(("wide", "narrow")),
        P(("wide", "narrow")),
        P(("wide", "narrow")),
        P(("wide", "narrow")),
        P(("wide", "narrow")),
        P(("wide", "narrow")),
        P(("wide", "narrow")),
        P(("wide", "narrow")),
        P(("wide", "narrow")),
    )
    return jax.shard_map(
        shards,
        mesh=mesh,
        in_specs=placed,
        out_specs=(
            P(("wide", "narrow"), None),
            P(("wide", "narrow"), None),
            P(("wide", "narrow"), None),
            P(("wide", "narrow"), None),
            P(("wide", "narrow"), None),
            P(("wide", "narrow"), None),
            P(("wide", "narrow"), None),
            P(("wide", "narrow"), None),
            P(("wide", "narrow")),
            P(("wide", "narrow")),
            P(("wide", "narrow")),
            P(("wide", "narrow")),
            P(("wide", "narrow")),
            P(("wide", "narrow")),
            P(("wide", "narrow")),
            P(("wide", "narrow")),
            P(("wide", "narrow")),
            P(("wide", "narrow")),
            P(),
        ),
        check_vma=False,
    )
```

profile of v0, /device:TPU:14, one launch (start us, length us, event | category | flops | bytes accessed | tf_op | source)
XLA Modules:
  0.0 1386.6 jit_solution(13215105580612590473)
XLA Ops:
  19.7 41.1 %all-reduce.20 = (bf16[1024]{0:T(1024)(128)(2,1)S(1)}, bf16[1024]{0:T(1024)(128)(2,1)S(1)}, bf16[1024]{0:T(1024)(128)(2,1)S(1)}, bf16[1024]{0:T(1024)(128)(2,1)S...) all-reduce(bf16[1024]{0:T(1024)(128)(2,1)S(1)} %dynamic-update-slic, ...), channel_id=1, replica_groups=mesh['wide'=16,'narrow'=2] {'wide','narrow'}, use_global_device_ids=true, to_apply=%add.1 | all-reduce | flops 9216 | bytes 36864
  62.6 28.8 %all-gather = bf16[32,1,128]{2,1,0:T(2,128)(2,1)S(1)} all-gather(bf16[1,1,128]{2,1,0:T(2,128)(2,1)} %bitcast.67), channel_id=1, replica_groups=mesh['wide'=16,'narrow'=2] {'wide','narrow'}, dimensions={0}, use_global_device_ids=true | all-gather | bytes 8448 | tf_op jit(solution)/shard_map/all_gather | solution.py:104
  92.0 1.5 fusion.21
  96.6 2.9 add_convert_fusion.1
  100.8 24.7 %all-gather.10.cloned.1.call-done = bf16[1024,1024]{1,0:T(8,128)(2,1)} async-done(((bf16[32,1024]{1,0:T(8,128)(2,1)}), bf16[1024,1024]{1,0:T(8,128)(2,1)}) %all-gather.10.cloned.1.call-update) | async-done | bytes 2097168 | tf_op jit(solution)/shard_map/all_gather | solution.py:94
  125.5 4.2 convolution_add_fusion.1
  129.7 1.9 copy.59
  131.7 52.0 %all-gather.12.cloned.1.call-done = bf16[1024,1024]{1,0:T(8,128)(2,1)} async-done(((bf16[32,1024]{1,0:T(8,128)(2,1)}), bf16[1024,1024]{1,0:T(8,128)(2,1)}) %all-gather.12.cloned.1.call-update) | async-done | bytes 2097168 | tf_op jit(solution)/shard_map/all_gather | solution.py:95
  183.7 4.2 convolution_add_fusion
  187.9 2.9 copy.60
  190.8 2.2 subtract_convert_fusion.1
  193.1 7.3 fusion.55
  200.4 8.4 fusion
  208.8 8.7 fusion.24
  217.5 24.1 %all-gather.14.cloned.1.call-done = bf16[1024,1024]{1,0:T(8,128)(2,1)} async-done(((bf16[32,1024]{1,0:T(8,128)(2,1)}), bf16[1024,1024]{1,0:T(8,128)(2,1)}) %all-gather.14.cloned.1.call-update) | async-done | bytes 2097168 | tf_op jit(solution)/shard_map/all_gather | solution.py:97
  241.6 3.3 multiply_reduce_fusion.9
  244.9 1.9 multiply_reduce_fusion.8
  246.8 74.6 %all-gather.16.cloned.1.call-done = bf16[1024,4096]{1,0:T(8,128)(2,1)} async-done(((bf16[32,4096]{1,0:T(8,128)(2,1)}), bf16[1024,4096]{1,0:T(8,128)(2,1)}) %all-gather.16.cloned.1.call-update) | async-done | bytes 8388624 | tf_op jit(solution)/shard_map/all_gather | solution.py:98
  321.4 11.8 fusion.38
  333.2 67.0 %all-gather.18.cloned.1.call-done = bf16[4096,1024]{1,0:T(8,128)(2,1)} async-done(((bf16[128,1024]{1,0:T(8,128)(2,1)}), bf16[4096,1024]{1,0:T(8,128)(2,1)}) %all-gather.18.cloned.1.call-update) | async-done | bytes 8388624 | tf_op jit(solution)/shard_map/all_gather | solution.py:99
  400.2 10.6 multiply_reduce_fusion.7
  410.9 1.5 multiply_reduce_fusion.1
  413.0 2.6 convert_reduce_fusion.1
  415.5 17.0 %convert_reduce_fusion = (f32[4096]{0:T(1024)}, bf16[512,4096]{1,0:T(8,128)(2,1)}) fusion(f32[512,4096]{1,0:T(8,128)} %fusion.38, f32[4096]{0:T(1024)S(1)} %bitcast.65, bf16[512,1024]{1,0:T(8,128)(2,1)S(1)} %get-tuple-element.48, bf16[4096,1024]{1,0:T(8,128)(2,1)} %all-gather.18.cloned.1.call-done), kind=kOutput, calls=%fused_computation.18 | convolution fusion | flops 4343197696 | bytes 22052864 | tf_op jit(solution)/shard_map/dot_general | solution.py:52
  432.5 7.4 multiply_reduce_fusion.2
  440.0 2.3 multiply_reduce_fusion.3
  444.6 3.3 fusion.58
  448.0 1.5 copy-done.11
  449.5 3.5 convolution_convert_fusion
  453.0 1.7 copy.62
  454.7 9.0 convert_reduce_fusion.3
  463.8 3.4 fusion.39
  467.3 9.0 multiply_reduce_fusion
  476.3 8.4 multiply_convert_fusion
  484.7 3.8 multiply_bitcast_fusion
  492.0 3.5 fusion.41
  495.8 3.4 fusion.43
  500.5 15.5 %fusion.48 = f32[4096,1024]{1,0:T(8,128)} fusion(bf16[512,1024]{1,0:T(8,128)(2,1)S(1)} %copy-done.23, f32[512,4096]{1,0:T(8,128)} %fusion.38, f32[4096]{0:T(1024)S(1)} %bitcast.66), kind=kOutput, calls=%fused_computation.114 | convolution fusion | flops 4315938816 | bytes 26230784 | tf_op jit(solution)/shard_map/dot_general | solution.py:46
  517.5 10.5 fusion.37
  529.2 3.0 fusion.56
  534.3 3.1 fusion.16
  537.4 41.4 %all-reduce.19 = (f32[1024]{0:T(1024)S(1)}, f32[1024]{0:T(1024)S(1)}, f32[1024]{0:T(1024)S(1)}, f32[1024]{0:T(1024)S(1)}, f32[4096]{0:T(1024)S(1)}, /*index=5*/f...) all-reduce(f32[1024]{0:T(1024)S(1)} %reduce_sum.252, ...), channel_id=8, replica_groups=mesh['wide'=16,'narrow'=2] {'wide','narrow'}, use_global_device_ids=true, to_apply=%region_19.20.clone | all-reduce | flops 13313 | bytes 106504
  585.3 3.5 fusion.20
  588.7 107.0 %reduce-scatter.11.cloned.1.call-done = f32[32,1024]{1,0:T(8,128)} async-done(((f32[1024,1024]{1,0:T(8,128)}), f32[32,1024]{1,0:T(8,128)}) %reduce-scatter.11.cloned.1.call-update) | async-done | bytes 131088 | tf_op jit(solution)/shard_map/reduce_scatter | solution.py:248
  695.8 140.0 %reduce-scatter.9.cloned.1.call-done = f32[32,1024]{1,0:T(8,128)} async-done(((f32[1024,1024]{1,0:T(8,128)}), f32[32,1024]{1,0:T(8,128)}) %reduce-scatter.9.cloned.1.call-update) | async-done | bytes 131088 | tf_op jit(solution)/shard_map/reduce_scatter | solution.py:247
  835.8 139.0 %reduce-scatter.7.cloned.1.call-done = f32[32,1024]{1,0:T(8,128)} async-done(((f32[1024,1024]{1,0:T(8,128)}), f32[32,1024]{1,0:T(8,128)}) %reduce-scatter.7.cloned.1.call-update) | async-done | bytes 131088 | tf_op jit(solution)/shard_map/reduce_scatter | solution.py:246
  974.8 216.3 %reduce-scatter.17.cloned.1.call-done = f32[128,1024]{1,0:T(8,128)} async-done(((f32[4096,1024]{1,0:T(8,128)}), f32[128,1024]{1,0:T(8,128)}) %reduce-scatter.17.cloned.1.call-update) | async-done | bytes 524304 | tf_op jit(solution)/shard_map/reduce_scatter | solution.py:257
  1191.1 187.2 %reduce-scatter.15.cloned.1.call-done = f32[32,4096]{1,0:T(8,128)} async-done(((f32[1024,4096]{1,0:T(8,128)}), f32[32,4096]{1,0:T(8,128)}) %reduce-scatter.15.cloned.1.call-update) | async-done | bytes 524304 | tf_op jit(solution)/shard_map/reduce_scatter | solution.py:256
  (196 shorter events, 37.9 us)
Async XLA Ops:
  7.2 89.1 %copy-start.30 = (s32[512]{0:T(512)S(1)}, s32[512]{0:T(512)}, u32[]{:S(2)}) copy-start(s32[512]{0:T(512)} %param.20) | copy-start | bytes 6148
  7.2 89.4 %copy-start.4 = (bf16[512,1024]{1,0:T(8,128)(2,1)S(1)}, bf16[512,1024]{1,0:T(8,128)(2,1)}, u32[]{:S(2)}) copy-start(bf16[512,1024]{1,0:T(8,128)(2,1)} %param.19) | copy-start | bytes 3145732
  7.2 89.4 %all-gather.8.cloned.1.call-start = ((), (), s32[]{:S(2)}) async-start(), calls=%async_computation.6 | async-start | bytes 2162688 | tf_op jit(solution)/shard_map/all_gather | solution.py:96
  7.9 117.6 %all-gather.10.cloned.1.call-start = ((), (), s32[]{:S(2)}) async-start(), calls=%async_computation.7 | async-start | bytes 2162688 | tf_op jit(solution)/shard_map/all_gather | solution.py:94
  8.7 175.0 %all-gather.12.cloned.1.call-start = ((), (), s32[]{:S(2)}) async-start(), calls=%async_computation.8 | async-start | bytes 2162688 | tf_op jit(solution)/shard_map/all_gather | solution.py:95
  9.4 232.2 %all-gather.14.cloned.1.call-start = ((), (), s32[]{:S(2)}) async-start(), calls=%async_computation.9 | async-start | bytes 2162688 | tf_op jit(solution)/shard_map/all_gather | solution.py:97
  10.0 311.4 %all-gather.16.cloned.1.call-start = ((), (), s32[]{:S(2)}) async-start(), calls=%async_computation.10 | async-start | bytes 8650752 | tf_op jit(solution)/shard_map/all_gather | solution.py:98
  10.6 389.6 %all-gather.18.cloned.1.call-start = ((), (), s32[]{:S(2)}) async-start(), calls=%async_computation.11 | async-start | bytes 8650752 | tf_op jit(solution)/shard_map/all_gather | solution.py:99
  11.2 577.6 %reduce-scatter.13.cloned.1.call-start = ((), (), s32[]{:S(2)}) async-start(), calls=%async_computation.15 | async-start | bytes 4325376 | tf_op jit(solution)/shard_map/reduce_scatter | solution.py:249
  94.1 31.5 %copy-start.35 = (f32[512]{0:T(512)}, f32[512]{0:T(512)S(1)}, u32[]{:S(2)}) copy-start(f32[512]{0:T(512)S(1)} %fusion.31) | copy-start | bytes 6148
  193.0 7.3 copy-start.12
  193.0 7.3 copy-start.14
  193.0 7.3 copy-start.16
  193.1 7.3 copy-start.18
  200.4 8.4 copy-start.8
  244.9 76.5 %copy-start.37 = (f32[1024]{0:T(1024)S(1)}, f32[1024]{0:T(1024)}, u32[]{:S(2)}) copy-start(f32[1024]{0:T(1024)} %convert_element_type.170) | copy-start | bytes 12292
  246.8 193.1 %copy-start.46 = (f32[512]{0:T(512)}, f32[512]{0:T(512)S(1)}, u32[]{:S(2)}) copy-start(f32[512]{0:T(512)S(1)} %fusion.33) | copy-start | bytes 6148
  321.4 78.8 %copy-start.43 = (f32[32,1,128]{2,1,0:T(1,128)S(1)}, f32[32,1,128]{2,1,0:T(1,128)}, u32[]{:S(2)}) copy-start(f32[32,1,128]{2,1,0:T(1,128)} %convert_element_type.198) | copy-start | bytes 49156
  400.2 10.7 copy-start.7
  400.2 10.7 copy-start.31
  400.2 10.7 copy-start.32
  413.0 19.6 %slice-start = ((s8[8388608]{0:T(1024)(128)(4,1)}), s8[4194304]{0:T(1024)(128)(4,1)S(1)}, s32[]{:S(2)}) async-start(s8[8388608]{0:T(1024)(128)(4,1)} %bitcast.68), calls=%async_computation.18 | async-start | bytes 8388608
  415.5 17.0 %copy-start.22 = (bf16[512,1024]{1,0:T(8,128)(2,1)}, bf16[512,1024]{1,0:T(8,128)(2,1)S(1)}, u32[]{:S(2)}) copy-start(bf16[512,1024]{1,0:T(8,128)(2,1)S(1)} %get-tuple-element.48) | copy-start | bytes 3145732
  415.5 17.0 %slice-start.1 = ((s8[8388608]{0:T(1024)(128)(4,1)}), s8[4194304]{0:T(1024)(128)(4,1)S(1)}, s32[]{:S(2)}) async-start(s8[8388608]{0:T(1024)(128)(4,1)} %bitcast.68), calls=%async_computation.19 | async-start | bytes 8388608
  442.3 2.3 copy-start.20
  447.9 247.8 %reduce-scatter.11.cloned.1.call-start = ((), (), s32[]{:S(2)}) async-start(), calls=%async_computation.14 | async-start | bytes 4325376 | tf_op jit(solution)/shard_map/reduce_scatter | solution.py:248
  449.5 17.8 %copy-start.28 = (f32[16,512]{1,0:T(8,128)}, f32[16,512]{1,0:T(8,128)S(1)}, u32[]{:S(2)}) copy-start(f32[16,512]{1,0:T(8,128)S(1)} %log_add_fusion) | copy-start | bytes 98308
  454.7 9.0 copy-start.6
  454.7 9.0 copy-start.36
  463.7 3.5 copy-start.9
  467.2 368.6 %reduce-scatter.9.cloned.1.call-start = ((), (), s32[]{:S(2)}) async-start(), calls=%async_computation.13 | async-start | bytes 4325376 | tf_op jit(solution)/shard_map/reduce_scatter | solution.py:247
  476.3 8.4 copy-start.17
  484.7 3.8 copy-start.13
  484.7 3.8 copy-start.15
  491.0 4.8 copy-start.26
  495.6 479.2 %reduce-scatter.7.cloned.1.call-start = ((), (), s32[]{:S(2)}) async-start(), calls=%async_computation.12 | async-start | bytes 4325376 | tf_op jit(solution)/shard_map/reduce_scatter | solution.py:246
  499.3 691.8 %reduce-scatter.17.cloned.1.call-start = ((), (), s32[]{:S(2)}) async-start(), calls=%async_computation.17 | async-start | bytes 17301504 | tf_op jit(solution)/shard_map/reduce_scatter | solution.py:257
  516.0 862.4 %reduce-scatter.15.cloned.1.call-start = ((), (), s32[]{:S(2)}) async-start(), calls=%async_computation.16 | async-start | bytes 17301504 | tf_op jit(solution)/shard_map/reduce_scatter | solution.py:256
  529.2 3.1 copy-start.25
  529.2 3.1 copy-start.51
  534.2 3.1 copy-start.39
  534.2 3.1 copy-start.40
  534.2 3.1 copy-start.41
  534.2 3.1 copy-start.42
  534.2 3.1 copy-start.45
  534.3 3.1 copy-start.50
  534.3 51.0 %copy-start.34 = (f32[512]{0:T(512)S(1)}, f32[512]{0:T(512)}, u32[]{:S(2)}) copy-start(f32[512]{0:T(512)} %copy-done.33) | copy-start | bytes 6148
  534.3 51.0 %copy-start.1 = (f32[512,1024]{1,0:T(8,128)S(1)}, f32[512,1024]{1,0:T(8,128)}, u32[]{:S(2)}) copy-start(f32[512,1024]{1,0:T(8,128)} %copy-done) | copy-start | bytes 6291460
  (18 other events, 24.8 us)
Sparse Core Ops, SparseCore 0:
  10.9 56.0 all-gather.7
  69.9 55.6 all-gather.9
  128.4 55.2 all-gather.11
  186.4 55.2 all-gather.13
  244.3 77.0 all-gather.15
  324.1 76.0 all-gather.17
  448.1 107.9 reduce-scatter.12
  558.9 136.8 reduce-scatter.10
  698.6 137.1 reduce-scatter.8
  838.5 136.2 reduce-scatter.6
  977.6 213.4 reduce-scatter.16
  1193.8 184.4 reduce-scatter.14
where the time goes:
time: 1390 us
  waiting for transfers between devices  1040 us (75%)
  matrix products  151 us (11%)
  blocking collectives  111 us (8%)
  other arithmetic  40.9 us (3%)
  local copies, waits for them, and re-layouts  29.8 us (2%)
  between operations  16.9 us (1%)
    reduce_scatter x1, waiting for transfers between devices, shards(): lax.psum_scatter(down_slope, ('wide', 'narrow'), scatter_dimension=0, til...  216 us
    reduce_scatter x1, waiting for transfers between devices, shards(): lax.psum_scatter(up_slope, ('wide', 'narrow'), scatter_dimension=0, tiled...  187 us
    reduce_scatter x1, waiting for transfers between devices, shards(): lax.psum_scatter(key_slope, ('wide', 'narrow'), scatter_dimension=0, tile...  140 us
    reduce_scatter x1, waiting for transfers between devices, shards(): lax.psum_scatter(query_slope, ('wide', 'narrow'), scatter_dimension=0, ti...  139 us
    reduce_scatter x1, waiting for transfers between devices, shards(): lax.psum_scatter(value_slope, ('wide', 'narrow'), scatter_dimension=0, ti...  107 us
    unnamed x2, blocking collectives  82.4 us
    all_gather x1, waiting for transfers between devices, shards(): lax.all_gather(upmatrix, ('wide', 'narrow'), axis=0, tiled=True)  74.6 us
    all_gather x1, waiting for transfers between devices, shards(): lax.all_gather(downmatrix, ('wide', 'narrow'), axis=0, tiled=True)  67 us
  transfers between devices with their start and end apart: 12, of which 10 were waited for; matrix products, arithmetic and copies ran while one was open for 12% of the time, Pallas kernels for 0%

commit v1 on v0

--- a/solution.py
+++ b/solution.py
@@ -90,12 +90,28 @@
     thirdgain,
     fourthgain,
 ):
+
+    def _make_cube(my_tile, bus_axis):
+        z_new = lax.psum(1, bus_axis)
+        tile_out, tall = (z_new, lax.axis_index(bus_axis))
+        outer, h_now = (my_tile, 1)
+        while h_now < tile_out:
+            block_list = []
+            for rr in tuple(range(tile_out)):
+                block_list.append((rr, rr ^ h_now))
+            kept_arr = lax.ppermute(outer, bus_axis, block_list)
+            side_arr = jnp.concatenate([outer, kept_arr], 0)
+            x_now = jnp.concatenate([kept_arr, outer], 0)
+            outer = jnp.where(tall & h_now == 0, side_arr, x_now)
+            h_now = 2 * h_now
+        return outer
+
     gathered = (
         lax.all_gather(querymat, ("wide", "narrow"), axis=0, tiled=True),
         lax.all_gather(keymat, ("wide", "narrow"), axis=0, tiled=True),
         lax.all_gather(valuemat, ("wide", "narrow"), axis=0, tiled=True),
         lax.all_gather(outmat, ("wide", "narrow"), axis=0, tiled=True),
-        lax.all_gather(upmatrix, ("wide", "narrow"), axis=0, tiled=True),
+        _make_cube(upmatrix, ("wide", "narrow")),
         lax.all_gather(downmatrix, ("wide", "narrow"), axis=0, tiled=True),
         lax.all_gather(querybias, ("wide", "narrow"), axis=0, tiled=True),
         lax.all_gather(keybias, ("wide", "narrow"), axis=0, tiled=True),

time: 1390 us -> 1520 us (1.094)
  waiting for transfers between devices: 1040 us -> 1110 us
  blocking collectives: 111 us -> 142 us
    all_gather x1, waiting for transfers between devices: 24.1 us -> 172 us  [shards(): lax.all_gather(outmat, ('wide', 'narrow'), axis=0, tiled=True)]
    all_gather x1, waiting for transfers between devices: 52 us -> 0.02 us  [shards(): lax.all_gather(keymat, ('wide', 'narrow'), axis=0, tiled=True)]
    ppermute x0 -> x5, waiting for transfers between devices: none -> 40.2 us  [_make_cube(): kept_arr = lax.ppermute(outer, bus_axis, block_list)]
    unnamed x2, blocking collectives: 82.4 us -> 114 us
    all_gather x1, waiting for transfers between devices: 74.6 us -> 46.2 us  [shards(): lax.all_gather(upmatrix, ('wide', 'narrow'), axis=0, tiled=True)]
    all_gather x1, waiting for transfers between devices: 24.7 us -> 0.01 us  [shards(): lax.all_gather(querymat, ('wide', 'narrow'), axis=0, tiled=True)]
  transfers between devices with their start and end apart: 12 -> 17, of which waited for: 10 -> 11; matrix products, arithmetic and copies ran while one was open for 12% -> 13% of each run, Pallas kernels for 0% -> 0%
where the time goes in v1:
time: 1520 us
  waiting for transfers between devices  1110 us (73%)
  matrix products  154 us (10%)
  blocking collectives  142 us (9%)
  other arithmetic  53.6 us (4%)
  local copies, waits for them, and re-layouts  23.9 us (2%)
  between operations  17.2 us (1%)
    reduce_scatter x1, waiting for transfers between devices, shards(): lax.psum_scatter(down_slope, ('wide', 'narrow'), scatter_dimension=0, til...  216 us
    reduce_scatter x1, waiting for transfers between devices, shards(): lax.psum_scatter(up_slope, ('wide', 'narrow'), scatter_dimension=0, tiled...  187 us
    all_gather x1, waiting for transfers between devices, shards(): lax.all_gather(outmat, ('wide', 'narrow'), axis=0, tiled=True)  172 us
    reduce_scatter x1, waiting for transfers between devices, shards(): lax.psum_scatter(key_slope, ('wide', 'narrow'), scatter_dimension=0, tile...  140 us
    reduce_scatter x1, waiting for transfers between devices, shards(): lax.psum_scatter(query_slope, ('wide', 'narrow'), scatter_dimension=0, ti...  140 us
    unnamed x2, blocking collectives  114 us
    reduce_scatter x1, waiting for transfers between devices, shards(): lax.psum_scatter(value_slope, ('wide', 'narrow'), scatter_dimension=0, ti...  106 us
    all_gather x1, waiting for transfers between devices, shards(): lax.all_gather(downmatrix, ('wide', 'narrow'), axis=0, tiled=True)  63.4 us
  transfers between devices with their start and end apart: 17, of which 11 were waited for; matrix products, arithmetic and copies ran while one was open for 13% of the time, Pallas kernels for 0%

profile of v1, /device:TPU:14, one launch (start us, length us, event | category | flops | bytes accessed | tf_op | source)
XLA Modules:
  0.0 1516.0 jit_solution(14649288851516226578)
XLA Ops:
  10.7 1.7 collective-permute-done
  14.2 13.9 collective-permute-done.1
  29.4 24.5 %collective-permute-done.2 = bf16[128,4096]{1,0:T(8,128)(2,1)} collective-permute-done((bf16[128,4096]{1,0:T(8,128)(2,1)S(1)}, bf16[128,4096]{1,0:T(8,128)(2,1)}, u32[]{:S(2)}, u32[]{:S(2)}) %collective-permute-start.2) | collective-permute-done | bytes 1048608 | tf_op jit(solution)/shard_map/ppermute | solution.py:102
  53.9 3.0 maximum_select_fusion.3
  59.8 72.6 %all-reduce.20 = (bf16[1024]{0:T(1024)(128)(2,1)S(1)}, bf16[1024]{0:T(1024)(128)(2,1)S(1)}, bf16[1024]{0:T(1024)(128)(2,1)S(1)}, bf16[1024]{0:T(1024)(128)(2,1)S...) all-reduce(bf16[1024]{0:T(1024)(128)(2,1)S(1)} %dynamic-update-slic, ...), channel_id=1, replica_groups=mesh['wide'=16,'narrow'=2] {'wide','narrow'}, use_global_device_ids=true, to_apply=%add.1 | all-reduce | flops 9216 | bytes 36864
  136.0 28.6 %all-gather = bf16[32,1,128]{2,1,0:T(2,128)(2,1)S(1)} all-gather(bf16[1,1,128]{2,1,0:T(2,128)(2,1)S(1)} %bitcast.66), channel_id=1, replica_groups=mesh['wide'=16,'narrow'=2] {'wide','narrow'}, dimensions={0}, use_global_device_ids=true | all-gather | bytes 8448 | tf_op jit(solution)/shard_map/all_gather | solution.py:120
  167.9 5.5 maximum_select_fusion.2
  173.3 8.6 collective-permute-start.4
  181.9 2.9 add_convert_fusion.1
  186.2 4.2 convolution_add_fusion.1
  190.4 1.9 copy.59
  192.3 4.2 convolution_add_fusion
  196.6 2.9 copy.60
  199.5 2.2 subtract_convert_fusion.1
  201.7 7.3 fusion.62
  209.1 8.4 fusion
  217.4 8.6 fusion.31
  226.1 172.5 %all-gather.14.cloned.1.call-done = bf16[1024,1024]{1,0:T(8,128)(2,1)} async-done(((bf16[32,1024]{1,0:T(8,128)(2,1)}), bf16[1024,1024]{1,0:T(8,128)(2,1)}) %all-gather.14.cloned.1.call-update) | async-done | bytes 2097168 | tf_op jit(solution)/shard_map/all_gather | solution.py:113
  398.5 3.3 multiply_reduce_fusion.9
  401.8 1.9 multiply_reduce_fusion.8
  403.8 11.1 fusion.11
  414.9 63.4 %all-gather.16.cloned.1.call-done = bf16[4096,1024]{1,0:T(8,128)(2,1)} async-done(((bf16[128,1024]{1,0:T(8,128)(2,1)}), bf16[4096,1024]{1,0:T(8,128)(2,1)}) %all-gather.16.cloned.1.call-update) | async-done | bytes 8388624 | tf_op jit(solution)/shard_map/all_gather | solution.py:115
  478.3 10.6 multiply_reduce_fusion.7
  491.0 4.6 convert_reduce_fusion.1
  496.6 14.2 convert_reduce_fusion
  510.9 46.2 %all-gather.18.cloned.1.call-done = bf16[1024,4096]{1,0:T(8,128)(2,1)} async-done(((bf16[32,4096]{1,0:T(8,128)(2,1)}), bf16[1024,4096]{1,0:T(8,128)(2,1)}) %all-gather.18.cloned.1.call-update) | async-done | bytes 8388624 | tf_op jit(solution)/shard_map/all_gather | solution.py:189
  557.1 10.7 multiply_reduce_fusion.2
  567.8 3.5 multiply_reduce_fusion.3
  573.6 3.3 fusion.65
  578.5 3.5 convolution_convert_fusion
  583.6 9.0 convert_reduce_fusion.3
  592.6 3.5 fusion.46
  596.2 9.0 multiply_reduce_fusion
  605.2 8.4 multiply_convert_fusion
  613.6 3.8 multiply_bitcast_fusion
  620.8 3.5 fusion.48
  624.4 3.4 fusion.50
  629.0 15.5 %fusion.55 = f32[4096,1024]{1,0:T(8,128)} fusion(bf16[512,1024]{1,0:T(8,128)(2,1)S(1)} %copy-done.23, f32[512,4096]{1,0:T(8,128)} %fusion.11, f32[4096]{0:T(1024)S(1)} %bitcast.65), kind=kOutput, calls=%fused_computation.126 | convolution fusion | flops 4315938816 | bytes 26230784 | tf_op jit(solution)/shard_map/dot_general | solution.py:46
  645.2 13.3 fusion.45
  659.7 3.1 fusion.63
  664.7 3.1 fusion.23
  667.8 41.3 %all-reduce.19 = (f32[1024]{0:T(1024)S(1)}, f32[1024]{0:T(1024)S(1)}, f32[1024]{0:T(1024)S(1)}, f32[1024]{0:T(1024)S(1)}, f32[4096]{0:T(1024)S(1)}, /*index=5*/f...) all-reduce(f32[1024]{0:T(1024)S(1)} %reduce_sum.252, ...), channel_id=8, replica_groups=mesh['wide'=16,'narrow'=2] {'wide','narrow'}, use_global_device_ids=true, to_apply=%region_19.20.clone | all-reduce | flops 13313 | bytes 106504
  715.6 3.5 fusion.27
  719.1 105.7 %reduce-scatter.11.cloned.1.call-done = f32[32,1024]{1,0:T(8,128)} async-done(((f32[1024,1024]{1,0:T(8,128)}), f32[32,1024]{1,0:T(8,128)}) %reduce-scatter.11.cloned.1.call-update) | async-done | bytes 131088 | tf_op jit(solution)/shard_map/reduce_scatter | solution.py:264
  824.8 139.9 %reduce-scatter.9.cloned.1.call-done = f32[32,1024]{1,0:T(8,128)} async-done(((f32[1024,1024]{1,0:T(8,128)}), f32[32,1024]{1,0:T(8,128)}) %reduce-scatter.9.cloned.1.call-update) | async-done | bytes 131088 | tf_op jit(solution)/shard_map/reduce_scatter | solution.py:263
  964.6 139.6 %reduce-scatter.7.cloned.1.call-done = f32[32,1024]{1,0:T(8,128)} async-done(((f32[1024,1024]{1,0:T(8,128)}), f32[32,1024]{1,0:T(8,128)}) %reduce-scatter.7.cloned.1.call-update) | async-done | bytes 131088 | tf_op jit(solution)/shard_map/reduce_scatter | solution.py:262
  1104.2 216.2 %reduce-scatter.17.cloned.1.call-done = f32[128,1024]{1,0:T(8,128)} async-done(((f32[4096,1024]{1,0:T(8,128)}), f32[128,1024]{1,0:T(8,128)}) %reduce-scatter.17.cloned.1.call-update) | async-done | bytes 524304 | tf_op jit(solution)/shard_map/reduce_scatter | solution.py:273
  1320.4 187.2 %reduce-scatter.15.cloned.1.call-done = f32[32,4096]{1,0:T(8,128)} async-done(((f32[1024,4096]{1,0:T(8,128)}), f32[32,4096]{1,0:T(8,128)}) %reduce-scatter.15.cloned.1.call-update) | async-done | bytes 524304 | tf_op jit(solution)/shard_map/reduce_scatter | solution.py:272
  (227 shorter events, 40.2 us)
Async XLA Ops:
  7.2 174.7 %all-gather.8.cloned.1.call-start = ((), (), s32[]{:S(2)}) async-start(), calls=%async_computation.6 | async-start | bytes 2162688 | tf_op jit(solution)/shard_map/all_gather | solution.py:112
  7.9 178.2 %all-gather.10.cloned.1.call-start = ((), (), s32[]{:S(2)}) async-start(), calls=%async_computation.7 | async-start | bytes 2162688 | tf_op jit(solution)/shard_map/all_gather | solution.py:110
  8.7 183.7 %all-gather.12.cloned.1.call-start = ((), (), s32[]{:S(2)}) async-start(), calls=%async_computation.8 | async-start | bytes 2162688 | tf_op jit(solution)/shard_map/all_gather | solution.py:111
  9.4 389.1 %all-gather.14.cloned.1.call-start = ((), (), s32[]{:S(2)}) async-start(), calls=%async_computation.9 | async-start | bytes 2162688 | tf_op jit(solution)/shard_map/all_gather | solution.py:113
  10.0 468.3 %all-gather.16.cloned.1.call-start = ((), (), s32[]{:S(2)}) async-start(), calls=%async_computation.10 | async-start | bytes 8650752 | tf_op jit(solution)/shard_map/all_gather | solution.py:115
  10.6 546.5 %all-gather.18.cloned.1.call-start = ((), (), s32[]{:S(2)}) async-start(), calls=%async_computation.11 | async-start | bytes 8650752 | tf_op jit(solution)/shard_map/all_gather | solution.py:189
  10.6 1.8 collective-permute-start
  13.6 14.5 collective-permute-start.1
  28.3 25.6 %collective-permute-start.2 = (bf16[128,4096]{1,0:T(8,128)(2,1)S(1)}, bf16[128,4096]{1,0:T(8,128)(2,1)}, u32[]{:S(2)}, u32[]{:S(2)}) collective-permute-start(bf16[128,4096]{1,0:T(8,128)(2,1)S(1)} %maximum_select_fusion.4), channel_id=1, source_target_pairs={{0,4},{1,5},{2,6},{3,7},{4,0},{5,1},{6,2},{7,3},{8,12},{9,13},{10,... | collective-permute-start | bytes 3145736 | tf_op jit(solution)/shard_map/ppermute | solution.py:102
  29.3 28.2 %copy-start.28 = (s32[512]{0:T(512)S(1)}, s32[512]{0:T(512)}, u32[]{:S(2)}) copy-start(s32[512]{0:T(512)} %param.20) | copy-start | bytes 6148
  29.3 28.4 %copy-start.54 = (bf16[32]{0:T(256)(128)(2,1)S(1)}, bf16[32]{0:T(256)(128)(2,1)}, u32[]{:S(2)}) copy-start(bf16[32]{0:T(256)(128)(2,1)} %param.37) | copy-start | bytes 196
  29.3 28.7 %copy-start.55 = (bf16[32]{0:T(256)(128)(2,1)S(1)}, bf16[32]{0:T(256)(128)(2,1)}, u32[]{:S(2)}) copy-start(bf16[32]{0:T(256)(128)(2,1)} %param.36) | copy-start | bytes 196
  29.3 28.9 %copy-start.56 = (bf16[32]{0:T(256)(128)(2,1)S(1)}, bf16[32]{0:T(256)(128)(2,1)}, u32[]{:S(2)}) copy-start(bf16[32]{0:T(256)(128)(2,1)} %param.31) | copy-start | bytes 196
  29.3 29.1 %copy-start.57 = (bf16[32]{0:T(256)(128)(2,1)S(1)}, bf16[32]{0:T(256)(128)(2,1)}, u32[]{:S(2)}) copy-start(bf16[32]{0:T(256)(128)(2,1)} %param.35) | copy-start | bytes 196
  29.3 29.3 %copy-start.58 = (bf16[32]{0:T(256)(128)(2,1)S(1)}, bf16[32]{0:T(256)(128)(2,1)}, u32[]{:S(2)}) copy-start(bf16[32]{0:T(256)(128)(2,1)} %param.28) | copy-start | bytes 196
  29.3 29.6 %copy-start.59 = (bf16[32]{0:T(256)(128)(2,1)S(1)}, bf16[32]{0:T(256)(128)(2,1)}, u32[]{:S(2)}) copy-start(bf16[32]{0:T(256)(128)(2,1)} %param.29) | copy-start | bytes 196
  29.3 29.8 %copy-start.60 = (bf16[32]{0:T(256)(128)(2,1)S(1)}, bf16[32]{0:T(256)(128)(2,1)}, u32[]{:S(2)}) copy-start(bf16[32]{0:T(256)(128)(2,1)} %param.34) | copy-start | bytes 196
  29.3 30.0 %copy-start.61 = (bf16[32]{0:T(256)(128)(2,1)S(1)}, bf16[32]{0:T(256)(128)(2,1)}, u32[]{:S(2)}) copy-start(bf16[32]{0:T(256)(128)(2,1)} %param.30) | copy-start | bytes 196
  29.3 30.2 %copy-start.62 = (bf16[32]{0:T(256)(128)(2,1)S(1)}, bf16[32]{0:T(256)(128)(2,1)}, u32[]{:S(2)}) copy-start(bf16[32]{0:T(256)(128)(2,1)} %param.33) | copy-start | bytes 196
  29.4 106.6 %copy-start.51 = (bf16[128]{0:T(256)(128)(2,1)S(1)}, bf16[128]{0:T(256)(128)(2,1)}, u32[]{:S(2)}) copy-start(bf16[128]{0:T(256)(128)(2,1)} %param.32) | copy-start | bytes 772
  29.4 135.8 %copy-start.2 = (bf16[512,1024]{1,0:T(8,128)(2,1)S(1)}, bf16[512,1024]{1,0:T(8,128)(2,1)}, u32[]{:S(2)}) copy-start(bf16[512,1024]{1,0:T(8,128)(2,1)} %param.19) | copy-start | bytes 3145732
  57.0 110.9 %collective-permute-start.3 = (bf16[256,4096]{1,0:T(8,128)(2,1)S(1)}, bf16[256,4096]{1,0:T(8,128)(2,1)}, u32[]{:S(2)}, u32[]{:S(2)}) collective-permute-start(bf16[256,4096]{1,0:T(8,128)(2,1)S(1)} %maximum_select_fusion.3), channel_id=1, source_target_pairs={{0,8},{1,9},{2,10},{3,11},{4,12},{5,13},{6,14},{7,15},{8,0},{9,1},... | collective-permute-start | bytes 6291464 | tf_op jit(solution)/shard_map/ppermute | solution.py:102
  57.4 661.6 %reduce-scatter.13.cloned.1.call-start = ((), (), s32[]{:S(2)}) async-start(), calls=%async_computation.15 | async-start | bytes 4325376 | tf_op jit(solution)/shard_map/reduce_scatter | solution.py:265
  167.8 14.1 copy-start.34
  173.3 230.4 %collective-permute-start.4 = (bf16[512,4096]{1,0:T(8,128)(2,1)}, bf16[512,4096]{1,0:T(8,128)(2,1)}, u32[]{:S(2)}, u32[]{:S(2)}) collective-permute-start(bf16[512,4096]{1,0:T(8,128)(2,1)} %maximum_select_fusion.2), channel_id=1, source_target_pairs={{0,16},{1,17},{2,18},{3,19},{4,20},{5,21},{6,22},{7,23},{8,24},{9,... | collective-permute-start | bytes 12582920 | tf_op jit(solution)/shard_map/ppermute | solution.py:102
  201.7 7.3 copy-start.12
  201.7 7.3 copy-start.14
  201.7 7.3 copy-start.16
  209.1 8.4 copy-start.8
  403.7 164.0 %copy-start.45 = (f32[512]{0:T(512)}, f32[512]{0:T(512)S(1)}, u32[]{:S(2)}) copy-start(f32[512]{0:T(512)S(1)} %fusion.40) | copy-start | bytes 6148
  403.7 74.5 %copy-start.29 = (f32[1024]{0:T(1024)S(1)}, f32[1024]{0:T(1024)}, u32[]{:S(2)}) copy-start(f32[1024]{0:T(1024)} %convert_element_type.174) | copy-start | bytes 12292
  403.8 74.5 %copy-start.42 = (f32[32,1,128]{2,1,0:T(1,128)S(1)}, f32[32,1,128]{2,1,0:T(1,128)}, u32[]{:S(2)}) copy-start(f32[32,1,128]{2,1,0:T(1,128)} %convert_element_type.198) | copy-start | bytes 49156
  478.3 10.7 copy-start.5
  478.3 10.7 copy-start.30
  478.3 10.7 copy-start.31
  489.0 7.6 copy-start.52
  557.1 10.7 copy-start.6
  577.0 247.8 %reduce-scatter.11.cloned.1.call-start = ((), (), s32[]{:S(2)}) async-start(), calls=%async_computation.14 | async-start | bytes 4325376 | tf_op jit(solution)/shard_map/reduce_scatter | solution.py:264
  578.5 17.6 %copy-start.26 = (f32[16,512]{1,0:T(8,128)}, f32[16,512]{1,0:T(8,128)S(1)}, u32[]{:S(2)}) copy-start(f32[16,512]{1,0:T(8,128)S(1)} %log_add_fusion) | copy-start | bytes 98308
  583.6 9.0 copy-start.4
  583.6 9.0 copy-start.35
  596.1 368.5 %reduce-scatter.9.cloned.1.call-start = ((), (), s32[]{:S(2)}) async-start(), calls=%async_computation.13 | async-start | bytes 4325376 | tf_op jit(solution)/shard_map/reduce_scatter | solution.py:263
  605.2 8.4 copy-start.17
  624.3 479.9 %reduce-scatter.7.cloned.1.call-start = ((), (), s32[]{:S(2)}) async-start(), calls=%async_computation.12 | async-start | bytes 4325376 | tf_op jit(solution)/shard_map/reduce_scatter | solution.py:262
  627.8 692.6 %reduce-scatter.17.cloned.1.call-start = ((), (), s32[]{:S(2)}) async-start(), calls=%async_computation.17 | async-start | bytes 17301504 | tf_op jit(solution)/shard_map/reduce_scatter | solution.py:273
  644.5 863.2 %reduce-scatter.15.cloned.1.call-start = ((), (), s32[]{:S(2)}) async-start(), calls=%async_computation.16 | async-start | bytes 17301504 | tf_op jit(solution)/shard_map/reduce_scatter | solution.py:272
  664.7 50.9 %copy-start.33 = (f32[512]{0:T(512)S(1)}, f32[512]{0:T(512)}, u32[]{:S(2)}) copy-start(f32[512]{0:T(512)} %copy-done.32) | copy-start | bytes 6148
  664.7 50.9 %copy-start.1 = (f32[512,1024]{1,0:T(8,128)S(1)}, f32[512,1024]{1,0:T(8,128)}, u32[]{:S(2)}) copy-start(f32[512,1024]{1,0:T(8,128)} %copy-done) | copy-start | bytes 6291460
  (32 other events, 70.4 us)
Sparse Core Ops, SparseCore 0:
  10.9 57.7 all-gather.7
  71.5 55.3 all-gather.9
  129.7 55.4 all-gather.11
  187.9 210.5 all-gather.13
  401.2 77.0 all-gather.15
  481.0 76.0 all-gather.17
  577.1 107.6 reduce-scatter.12
  687.7 137.0 reduce-scatter.10
  827.6 136.9 reduce-scatter.8
  967.3 136.8 reduce-scatter.6
  1107.1 213.2 reduce-scatter.16
  1323.2 184.4 reduce-scatter.14
